TPU v7x, 32 devices: a whole 2x2x4 slice. The times are simulated.
32 devices in a mesh: member: 2 (over core), grid: 16 (over z, y, x).
Axes of the slice: x: 2, y: 2, z: 4, core: 2. Of those that a mesh axis runs over, the one named last changes fastest.
Arguments:
- latent: bfloat16 [4, 32768, 512], P('member', 'grid'), may hold values from -80 to 80
- block_pick: int32 [16, 16], P('grid'), may hold values from 0 to 15
- obs_weight: bfloat16 [16, 16, 128, 128], P('grid'), may hold values from 0.0099487305 to 1
- obs_value: float32 [16, 16, 128, 128], P('grid'), may hold values from -6 to 6
- obs_count: int32 [16, 16], P('grid'), may hold values from 0 to 128, as said below
- w_in: bfloat16 [512, 512], replicated, may hold values from -0.25 to 0.25
- b_in: float32 [512], replicated, may hold values from -3 to 3
- w_out: bfloat16 [512, 128], replicated, may hold values from -0.25 to 0.25
- b_out: float32 [128], replicated, may hold values from -3 to 3
Outputs:
- latent_grad: float32 [4, 32768, 512], P('member', 'grid')
- loss_value: float32 [], replicated
Inputs may be any that keep to these rules, and one draw needn't show every extreme that they name: Entry [d, j] counts the live observations of those slots; the live ones are the first slots, k < obs_count[d, j].
All inputs are finite; a program needn't handle non-finite values.
Results may differ from a plain program's by a relative error of at most 0.0041.
Values may be sent and summed in bfloat16 or wider, within the bound.
A program may use at most 128 MiB of HBM per device.

v0:
```python
import jax
import jax.numpy as jnp
from jax import lax
from jax.sharding import PartitionSpec as P

SOFTEN = 0.1


def smooth_abs(value):
    return jnp.sqrt(value * value + SOFTEN * SOFTEN)


def silu_slope(pre_act):
    sigmoid_value = jax.nn.sigmoid(pre_act)
    return sigmoid_value * (1.0 + pre_act * (1.0 - sigmoid_value))


def per_device(latent, block_pick, obs_weight, obs_value, obs_count, w_in, b_in, w_out, b_out):
    members_here, points, feature_width = latent.shape
    peer_count = lax.axis_size("grid")
    slot_count = obs_weight.shape[2]
    block_size = obs_weight.shape[3]
    channels = obs_value.shape[3]
    members_all = members_here * lax.axis_size("member")
    block_count = points // block_size
    local_blocks = latent.reshape(members_here, block_count, block_size, feature_width)
    picked_ids = block_pick[0]
    block_onehot = (
        picked_ids[:, None] == jnp.arange(block_count, dtype=jnp.int32)[None, :]
    ).astype(jnp.bfloat16)
    weight_sum = jnp.sum(obs_weight[0], axis=2, keepdims=True, dtype=jnp.float32)
    norm_weight = (obs_weight[0] / weight_sum).astype(jnp.bfloat16)
    picked = local_blocks[:, picked_ids]
    interp = jnp.einsum(
        "jkp,mjpc->mjkc",
        norm_weight,
        lax.all_to_all(picked, "grid", split_axis=1, concat_axis=1, tiled=True),
        preferred_element_type=jnp.float32,
    ).astype(jnp.bfloat16)
    flat_rows = interp.reshape(members_here * peer_count * slot_count, feature_width)
    pre_act = jnp.dot(flat_rows, w_in, preferred_element_type=jnp.float32) + b_in
    hidden = jax.nn.silu(pre_act).astype(jnp.bfloat16)
    predicted = jnp.dot(hidden, w_out, preferred_element_type=jnp.float32) + b_out
    predicted = predicted.reshape(members_here, peer_count, slot_count, channels)
    all_members = lax.all_gather(predicted, "member", axis=0, tiled=True)
    target = obs_value[0]
    live_mask = (jnp.arange(slot_count, dtype=jnp.int32)[None, :] < obs_count[0][:, None]).astype(
        jnp.float32
    )
    obs_diff = predicted - target[None]
    pair_diff = predicted[:, None] - all_members[None]
    per_obs = smooth_abs(obs_diff) / members_all - jnp.sum(smooth_abs(pair_diff), axis=1) / (
        2.0 * members_all * (members_all - 1)
    )
    loss_part = jnp.sum(per_obs * live_mask[None, :, :, None])
    live_count = jnp.sum(live_mask)
    live_total = lax.psum(live_count, "grid")
    loss_total = lax.psum(loss_part, ("member", "grid"))
    loss_value = loss_total / (channels * live_total)
    grad_scale = peer_count * peer_count * slot_count / live_total
    slope_obs = obs_diff / smooth_abs(obs_diff)
    slope_pair = jnp.sum(pair_diff / smooth_abs(pair_diff), axis=1)
    grad_pred = (
        grad_scale
        * live_mask[None, :, :, None]
        * (slope_obs / members_all - slope_pair / (members_all * (members_all - 1.0)))
    ).astype(jnp.bfloat16)
    grad_hidden = jnp.einsum(
        "rv,hv->rh", grad_pred.reshape(-1, channels), w_out, preferred_element_type=jnp.float32
    )
    grad_act = (grad_hidden * silu_slope(pre_act)).astype(jnp.bfloat16)
    grad_interp = jnp.einsum(
        "rh,ch->rc", grad_act, w_in, preferred_element_type=jnp.float32
    ).astype(jnp.bfloat16)
    grad_interp = grad_interp.reshape(members_here, peer_count, slot_count, feature_width)
    contribution = jnp.einsum(
        "jkp,mjkc->mjpc", norm_weight, grad_interp, preferred_element_type=jnp.float32
    ).astype(jnp.bfloat16)
    returned = lax.all_to_all(contribution, "grid", split_axis=1, concat_axis=1, tiled=True)
    summed = jnp.einsum("mdpc,db->mbpc", returned, block_onehot, preferred_element_type=jnp.float32)
    latent_grad = summed.reshape(members_here, points, feature_width)
    return (latent_grad, loss_value)


def solution(mesh):
    in_specs = (
        P("member", "grid", None),
        P("grid", None),
        P("grid", None, None, None),
        P("grid", None, None, None),
        P("grid", None),
        P(),
        P(),
        P(),
        P(),
    )
    out_specs = (P("member", "grid", None), P())
    return jax.shard_map(
        per_device, mesh=mesh, in_specs=in_specs, out_specs=out_specs, check_vma=False
    )
```

profile of v0, /device:TPU:0, one launch (start us, length us, event | category | flops | bytes accessed | tf_op | source)
XLA Modules:
  0.0 332.6 jit_solution(2911062721672756190)
XLA Ops:
  7.2 0.0 copy-start
  7.2 0.7 fusion.26
  7.9 5.0 %gather_fusion = bf16[16,2,128,512]{3,2,1,0:T(8,128)(2,1)} fusion(bf16[2,16,128,512]{3,2,1,0:T(8,128)(2,1)} %bitcast.72, s32[1024]{0:T(1024)S(1)} %pad_clamp_fusion), kind=kCustom, calls=%fused_computation | custom fusion | bytes 8388672 | tf_op jit(solution)/shard_map/gather | solution.py:33
  12.9 0.0 copy-start.4
  12.9 8.5 %all-to-all-start = ((bf16[2,16,128,512]{3,2,0,1:T(8,128)(2,1)}), bf16[2,16,128,512]{3,2,0,1:T(8,128)(2,1)}, u32[]{:S(2)}, u32[]{:S(2)}) async-start(bf16[2,16,128,512]{3,2,0,1:T(8,128)(2,1)} %bitcast.70), calls=%async_computation | async-start | bytes 8388608 | tf_op jit(solution)/shard_map/all_to_all | solution.py:37
  21.5 0.0 all-gather.2.cloned.1.call-start
  21.5 0.0 copy-done.4
  21.5 0.2 convert_reduce_fusion
  21.7 79.5 %all-to-all-done = bf16[2,16,128,512]{3,2,0,1:T(8,128)(2,1)} async-done(((bf16[2,16,128,512]{3,2,0,1:T(8,128)(2,1)}), bf16[2,16,128,512]{3,2,0,1:T(8,128)(2,1)}, u32[]{:S(2)}, u32[]{:S(2)}) %all-to-all-start) | async-done | bytes 4194336 | tf_op jit(solution)/shard_map/all_to_all | solution.py:37
  101.2 3.5 %convert_bitcast_fusion.1 = bf16[2,16,128,512]{3,2,0,1:T(8,128)(2,1)S(1)} fusion(bf16[2,16,128,512]{3,2,0,1:T(8,128)(2,1)} %all-to-all-done, bf16[1,16,128,128]{3,2,1,0:T(8,128)(2,1)S(1)} %copy-done.4, f32[16,128]{1,0:T(8,128)S(1)} %convert_reduce_fusion), kind=kOutput, calls=%fused_computation.17 | convolution fusion | flops 539754496 | bytes 8921088 | tf_op jit(solution)/shard_map/jkp,mjpc->mjkc/dot_general | solution.py:34
  104.7 0.4 copy.18
  105.1 0.0 copy-done
  105.1 0.0 copy-start.8
  105.1 0.0 copy-start.9
  105.2 0.0 copy-start.10
  105.2 2.4 fusion.31
  107.6 0.0 copy-done.8
  107.6 0.0 copy-done.9
  107.6 0.0 copy-done.10
  107.6 0.0 copy-start.3
  107.6 0.0 copy-start.6
  107.7 4.1 %convolution_add_fusion = f32[4096,128]{1,0:T(8,128)} fusion(bf16[512,128]{1,0:T(8,128)(2,1)S(1)} %copy-done.8, f32[4096,512]{1,0:T(8,128)S(1)} %fusion.31, f32[512]{0:T(512)S(1)} %copy-done.9, f32[128]{0:T(128)S(1)} %copy-done.10), kind=kOutput, calls=%fused_computation.11 | convolution fusion | flops 549978112 | bytes 10619392 | tf_op jit(solution)/shard_map/dot_general | solution.py:43
  111.7 0.0 copy-done.3
  111.7 0.0 all-gather.2.cloned.1.call-update
  111.8 0.0 copy-done.6
  111.8 0.7 fusion.25
  112.4 55.0 %psum.14 = f32[]{:T(128)} all-reduce(f32[]{:T(128)} %fusion.25), channel_id=1, replica_groups=mesh['member'=2,'grid'=16] {'grid'}, use_global_device_ids=true, to_apply=%region_1.2 | all-reduce | flops 1 | bytes 8 | tf_op jit(solution)/shard_map/psum | solution.py:57
  168.1 0.1 fusion.21
  168.2 0.1 fusion.20
  168.2 0.0 all-gather.2.cloned.1.call-done
  168.2 7.3 %fusion.2 = (f32[2,16,128,128]{3,2,1,0:T(8,128)S(1)}, f32[2,16,128,128]{3,2,1,0:T(8,128)S(1)}) fusion(f32[4,16,128,128]{3,2,1,0:T(8,128)} %all-gather.2.cloned.1.call-done, f32[2,16,128,128]{3,2,1,0:T(8,128)} %bitcast.68), kind=kLoop, calls=%fused_computation.5 | loop fusion | flops 11534336 | bytes 10485760 | tf_op jit(solution)/shard_map/reduce_sum | solution.py:52
  175.5 0.0 copy-start.2
  175.5 0.0 copy-start.5
  175.6 0.7 broadcast_multiply_fusion
  176.3 0.8 copy-done.2
  177.1 0.3 copy-done.5
  177.4 2.5 fusion.14
  179.9 8.6 %convolution_convert_fusion = bf16[4096,512]{1,0:T(8,128)(2,1)} fusion(bf16[512,512]{1,0:T(8,128)(2,1)S(1)} %copy-done, f32[4096,512]{1,0:T(8,128)} %copy-done.3, bf16[4096,128]{1,0:T(8,128)(2,1)S(1)} %get-tuple-element.5, bf16[512,128]{1,0:T(8,128)(2,1)S(1)} %copy-done.8, f32[512]{0:T(512)S(1)} %copy-done.9), kind=kOutput, calls=%fused_computation.10 | convolution fusion | flops 2707423232 | bytes 14288896 | tf_op jit(solution)/shard_map/rh,ch->rc/dot_general | solution.py:72
  188.6 5.9 %convert_bitcast_fusion = bf16[2,16,128,512]{2,3,0,1:T(8,128)(2,1)} fusion(bf16[2,16,128,512]{3,2,1,0:T(8,128)(2,1)} %bitcast.80, bf16[1,16,128,128]{3,2,1,0:T(8,128)(2,1)S(1)} %copy-done.4, f32[16,128]{1,0:T(8,128)S(1)} %convert_reduce_fusion), kind=kOutput, calls=%fused_computation.16 | convolution fusion | flops 539754496 | bytes 8921088 | tf_op jit(solution)/shard_map/jkp,mjkc->mjpc/dot_general | solution.py:76
  194.4 6.4 %copy.20 = bf16[2,16,128,512]{3,2,0,1:T(8,128)(2,1)} copy(bf16[2,16,128,512]{2,3,0,1:T(8,128)(2,1)} %convert_bitcast_fusion) | data formatting | bytes 8388608 | tf_op jit(solution)/shard_map/convert_element_type | solution.py:78
  200.8 4.7 %all-to-all-start.1 = ((bf16[2,16,128,512]{3,2,0,1:T(8,128)(2,1)}), bf16[2,16,128,512]{3,2,0,1:T(8,128)(2,1)}, u32[]{:S(2)}, u32[]{:S(2)}) async-start(bf16[2,16,128,512]{3,2,0,1:T(8,128)(2,1)} %copy.20), calls=%async_computation.1 | async-start | bytes 8388608 | tf_op jit(solution)/shard_map/all_to_all | solution.py:79
  206.1 104.7 %psum.15 = f32[]{:T(128)} all-reduce(f32[]{:T(128)} %get-tuple-element.4), channel_id=1, replica_groups=mesh['member'=2,'grid'=16] {'member','grid'}, use_global_device_ids=true, to_apply=%region_6.7 | all-reduce | flops 1 | bytes 8 | tf_op jit(solution)/shard_map/psum | solution.py:58
  311.6 0.0 all-to-all-done.1
  311.6 0.0 copy-done.7
  311.6 4.7 %fusion.8 = f32[2,16,128,512]{3,1,2,0:T(8,128)S(1)} fusion(bf16[2,16,128,512]{3,2,0,1:T(8,128)(2,1)} %all-to-all-done.1, s32[16]{0:T(128)S(1)} %bitcast.79), kind=kOutput, calls=%fused_computation.18 | convolution fusion | flops 67109120 | bytes 12582976 | tf_op jit(solution)/shard_map/mdpc,db->mbpc/dot_general | solution.py:80
  316.3 0.0 copy-start.1
  316.3 8.3 %copy.22 = f32[2,16,128,512]{3,2,1,0:T(8,128)} copy(f32[2,16,128,512]{3,1,2,0:T(8,128)S(1)} %fusion.8) | data formatting | bytes 16777216 | tf_op jit(solution)/shard_map/mdpc,db->mbpc/transpose | solution.py:80
  324.6 0.0 copy-done.1
  (4 shorter events, 0.0 us)
Async XLA Ops:
  7.2 98.0 %copy-start = (bf16[512,512]{1,0:T(8,128)(2,1)S(1)}, bf16[512,512]{1,0:T(8,128)(2,1)}, u32[]{:S(2)}) copy-start(bf16[512,512]{1,0:T(8,128)(2,1)} %param.14) | copy-start | bytes 1572868
  12.9 8.6 %copy-start.4 = (bf16[1,16,128,128]{3,2,1,0:T(8,128)(2,1)S(1)}, bf16[1,16,128,128]{3,2,1,0:T(8,128)(2,1)}, u32[]{:S(2)}) copy-start(bf16[1,16,128,128]{3,2,1,0:T(8,128)(2,1)} %param.11) | copy-start | bytes 1572868
  12.9 88.3 %all-to-all-start = ((bf16[2,16,128,512]{3,2,0,1:T(8,128)(2,1)}), bf16[2,16,128,512]{3,2,0,1:T(8,128)(2,1)}, u32[]{:S(2)}, u32[]{:S(2)}) async-start(bf16[2,16,128,512]{3,2,0,1:T(8,128)(2,1)} %bitcast.70), calls=%async_computation | async-start | bytes 8388608 | tf_op jit(solution)/shard_map/all_to_all | solution.py:37
  21.5 146.8 %all-gather.2.cloned.1.call-start = ((), (), s32[]{:S(2)}) async-start(), calls=%async_computation.2 | async-start | bytes 6291456 | tf_op jit(solution)/shard_map/all_gather | solution.py:45
  105.1 2.5 copy-start.8
  105.1 2.5 copy-start.9
  105.2 2.5 copy-start.10
  107.6 4.1 %copy-start.3 = (f32[4096,512]{1,0:T(8,128)}, f32[4096,512]{1,0:T(8,128)S(1)}, u32[]{:S(2)}) copy-start(f32[4096,512]{1,0:T(8,128)S(1)} %fusion.31) | copy-start | bytes 25165828
  107.6 4.1 %copy-start.6 = (s32[1,16]{1,0:T(1,128)S(1)}, s32[1,16]{1,0:T(1,128)}, u32[]{:S(2)}) copy-start(s32[1,16]{1,0:T(1,128)} %param.13) | copy-start | bytes 196
  175.5 1.6 copy-start.2
  175.5 1.8 copy-start.5
  200.8 110.7 %copy-start.7 = (s32[1,16]{1,0:T(1,128)S(1)}, s32[1,16]{1,0:T(1,128)}, u32[]{:S(2)}) copy-start(s32[1,16]{1,0:T(1,128)} %param.10) | copy-start | bytes 196
  200.8 110.7 %all-to-all-start.1 = ((bf16[2,16,128,512]{3,2,0,1:T(8,128)(2,1)}), bf16[2,16,128,512]{3,2,0,1:T(8,128)(2,1)}, u32[]{:S(2)}, u32[]{:S(2)}) async-start(bf16[2,16,128,512]{3,2,0,1:T(8,128)(2,1)} %copy.20), calls=%async_computation.1 | async-start | bytes 8388608 | tf_op jit(solution)/shard_map/all_to_all | solution.py:79
  316.3 8.3 %copy-start.1 = (bf16[512,512]{1,0:T(8,128)(2,1)S(1)}, bf16[512,512]{1,0:T(8,128)(2,1)}, u32[]{:S(2)}) copy-start(bf16[512,512]{1,0:T(8,128)(2,1)} %param.14) | copy-start | bytes 1572868
Sparse Core Ops, SparseCore 0:
  111.9 28.1 all-gather.1
where the time goes:
time: 333 us
  blocking collectives  160 us (48%)
  waiting for transfers between devices  79.5 us (24%)
  matrix products  29.2 us (9%)
  local copies, waits for them, and re-layouts  21.3 us (6%)
  between operations  17.4 us (5%)
  starting transfers between devices  13.2 us (4%)
  other arithmetic  12.3 us (4%)
    psum x1, blocking collectives, per_device(): loss_total = lax.psum(loss_part, ('member', 'grid'))  105 us
    all_to_all x1, waiting for transfers between devices, per_device(): lax.all_to_all(picked, 'grid', split_axis=1, concat_axis=1, tiled=True)  79.5 us
    psum x1, blocking collectives, per_device(): live_total = lax.psum(live_count, 'grid')  55 us
    dot_general x1, matrix products, per_device(): jnp.einsum('rh,ch->rc', grad_act, w_in, preferred_element_type=jnp.float32)  8.64 us
    all_to_all x1, starting transfers between devices, per_device(): lax.all_to_all(picked, 'grid', split_axis=1, concat_axis=1, tiled=True)  8.52 us
    transpose x1, local copies, waits for them, and re-layouts, per_device(): jnp.einsum('mdpc,db->mbpc', returned, block_onehot, preferred_element_typ...  8.25 us
    reduce_sum x1, other arithmetic, per_device(): jnp.sum(smooth_abs(pair_diff), axis=1)  7.3 us
  transfers between devices with their start and end apart: 3, of which 1 were waited for; matrix products, arithmetic and copies ran while one was open for 0% of the time, Pallas kernels for 0%

commit v1 on v0

--- a/solution.py
+++ b/solution.py
@@ -34,7 +34,12 @@
     interp = jnp.einsum(
         "jkp,mjpc->mjkc",
         norm_weight,
-        lax.all_to_all(picked, "grid", split_axis=1, concat_axis=1, tiled=True),
+        jnp.concatenate(
+            lax.all_to_all(
+                jnp.stack(jnp.split(picked, lax.axis_size("grid"), axis=1)), "grid", 0, 0
+            ),
+            axis=1,
+        ),
         preferred_element_type=jnp.float32,
     ).astype(jnp.bfloat16)
     flat_rows = interp.reshape(members_here * peer_count * slot_count, feature_width)

time: 333 us -> 353 us (1.060)
  local copies, waits for them, and re-layouts: 21.3 us -> 40.6 us
    unnamed x22 -> x39, local copies, waits for them, and re-layouts: 1.14 us -> 19.7 us
where the time goes in v1:
time: 353 us; the launch traced here: 352 us
  blocking collectives  160 us (45%)
  waiting for transfers between devices  79.5 us (23%)
  local copies, waits for them, and re-layouts  40.6 us (12%)
  matrix products  29.2 us (8%)
  between operations  17.4 us (5%)
  starting transfers between devices  13.2 us (4%)
  other arithmetic  12.3 us (3%)
    psum x1, blocking collectives, per_device(): loss_total = lax.psum(loss_part, ('member', 'grid'))  105 us
    all_to_all x1, waiting for transfers between devices, per_device(): lax.all_to_all(jnp.stack(jnp.split(picked, lax.axis_size('grid'), axis=1)...  79.5 us
    psum x1, blocking collectives, per_device(): live_total = lax.psum(live_count, 'grid')  55 us
    unnamed x39, local copies, waits for them, and re-layouts  19.7 us
    dot_general x1, matrix products, per_device(): jnp.einsum('rh,ch->rc', grad_act, w_in, preferred_element_type=jnp.float32)  8.64 us
    all_to_all x1, starting transfers between devices, per_device(): lax.all_to_all(jnp.stack(jnp.split(picked, lax.axis_size('grid'), axis=1)...  8.52 us
    transpose x1, local copies, waits for them, and re-layouts, per_device(): jnp.einsum('mdpc,db->mbpc', returned, block_onehot, preferred_element_typ...  8.25 us
    reduce_sum x1, other arithmetic, per_device(): jnp.sum(smooth_abs(pair_diff), axis=1)  7.3 us
  transfers between devices with their start and end apart: 3, of which 1 were waited for; matrix products, arithmetic and copies ran while one was open for 0% of the time, Pallas kernels for 0%

profile of v1, /device:TPU:0, one launch (start us, length us, event | category | flops | bytes accessed | tf_op | source)
XLA Modules:
  0.0 351.9 jit_solution(15275541808133023179)
XLA Ops:
  7.2 0.0 copy-start
  7.2 0.7 fusion.46
  7.9 5.0 %gather_fusion = bf16[16,2,128,512]{3,2,1,0:T(8,128)(2,1)} fusion(bf16[2,16,128,512]{3,2,1,0:T(8,128)(2,1)} %bitcast.159, s32[1024]{0:T(1024)S(1)} %pad_clamp_fusion), kind=kCustom, calls=%fused_computation | custom fusion | bytes 8388672 | tf_op jit(solution)/shard_map/gather | solution.py:33
  12.9 1.8 fusion.39
  14.7 1.7 fusion.38
  16.4 1.7 fusion.37
  18.1 1.7 fusion.36
  19.7 1.7 fusion.35
  21.4 1.7 fusion.34
  23.1 1.7 fusion.33
  24.8 1.7 fusion.32
  26.5 0.7 fusion.31
  27.2 0.7 fusion.30
  27.9 0.7 fusion.29
  28.7 0.7 fusion.28
  29.4 0.7 fusion.27
  30.1 0.7 fusion.26
  30.8 0.7 fusion.25
  31.5 0.7 fusion.24
  32.3 8.5 %all-to-all-start = ((bf16[16,2,1,128,512]{4,3,1,2,0:T(8,128)(2,1)}), bf16[16,2,1,128,512]{4,3,1,2,0:T(8,128)(2,1)}, u32[]{:S(2)}, u32[]{:S(2)}) async-start(bf16[16,2,1,128,512]{4,3,1,2,0:T(8,128)(2,1)} %fusion.24), calls=%async_computation | async-start | bytes 8388608 | tf_op jit(solution)/shard_map/all_to_all | solution.py:38
  40.8 0.0 all-gather.2.cloned.1.call-start
  40.9 0.2 convert_reduce_fusion
  41.1 79.5 %all-to-all-done = bf16[16,2,1,128,512]{4,3,1,2,0:T(8,128)(2,1)} async-done(((bf16[16,2,1,128,512]{4,3,1,2,0:T(8,128)(2,1)}), bf16[16,2,1,128,512]{4,3,1,2,0:T(8,128)(2,1)}, u32[]{:S(2)}, u32[]{:S(2)}) %all-to-all-start) | async-done | bytes 4194336 | tf_op jit(solution)/shard_map/all_to_all | solution.py:38
  120.6 3.5 convert_bitcast_fusion.1
  124.1 0.4 copy.50
  124.5 0.0 copy-start.9
  124.5 0.0 copy-start.10
  124.5 0.0 copy-start.11
  124.5 2.4 fusion.51
  127.0 0.0 copy-start.4
  127.0 4.1 %convolution_add_fusion = f32[4096,128]{1,0:T(8,128)} fusion(bf16[512,128]{1,0:T(8,128)(2,1)S(1)} %copy-done.9, f32[4096,512]{1,0:T(8,128)S(1)} %fusion.51, f32[512]{0:T(512)S(1)} %copy-done.10, f32[128]{0:T(128)S(1)} %copy-done.11), kind=kOutput, calls=%fused_computation.11 | convolution fusion | flops 549978112 | bytes 10619392 | tf_op jit(solution)/shard_map/dot_general | solution.py:48
  131.1 0.0 all-gather.2.cloned.1.call-update
  131.1 0.7 fusion.45
  131.8 55.0 %psum.14 = f32[]{:T(128)} all-reduce(f32[]{:T(128)} %fusion.45), channel_id=1, replica_groups=mesh['member'=2,'grid'=16] {'grid'}, use_global_device_ids=true, to_apply=%region_1.2 | all-reduce | flops 1 | bytes 8 | tf_op jit(solution)/shard_map/psum | solution.py:62
  187.4 0.1 fusion.41
  187.5 0.1 fusion.40
  187.6 7.3 %fusion.2 = (f32[2,16,128,128]{3,2,1,0:T(8,128)S(1)}, f32[2,16,128,128]{3,2,1,0:T(8,128)S(1)}) fusion(f32[4,16,128,128]{3,2,1,0:T(8,128)} %all-gather.2.cloned.1.call-done, f32[2,16,128,128]{3,2,1,0:T(8,128)} %bitcast.140), kind=kLoop, calls=%fused_computation.5 | loop fusion | flops 11534336 | bytes 10485760 | tf_op jit(solution)/shard_map/reduce_sum | solution.py:57
  194.9 0.7 broadcast_multiply_fusion
  195.7 0.8 copy-done.2
  196.5 0.3 copy-done.6
  196.8 2.5 fusion.18
  199.3 8.6 %convolution_convert_fusion = bf16[4096,512]{1,0:T(8,128)(2,1)} fusion(bf16[512,512]{1,0:T(8,128)(2,1)S(1)} %copy-done, f32[4096,512]{1,0:T(8,128)} %copy-done.4, bf16[4096,128]{1,0:T(8,128)(2,1)S(1)} %get-tuple-element.5, bf16[512,128]{1,0:T(8,128)(2,1)S(1)} %copy-done.9, f32[512]{0:T(512)S(1)} %copy-done.10), kind=kOutput, calls=%fused_computation.10 | convolution fusion | flops 2707423232 | bytes 14288896 | tf_op jit(solution)/shard_map/rh,ch->rc/dot_general | solution.py:77
  207.9 5.9 %convert_bitcast_fusion = bf16[2,16,128,512]{2,3,0,1:T(8,128)(2,1)} fusion(bf16[2,16,128,512]{3,2,1,0:T(8,128)(2,1)} %bitcast.167, bf16[1,16,128,128]{3,2,1,0:T(8,128)(2,1)S(1)} %copy-done.5, f32[16,128]{1,0:T(8,128)S(1)} %convert_reduce_fusion), kind=kOutput, calls=%fused_computation.18 | convolution fusion | flops 539754496 | bytes 8921088 | tf_op jit(solution)/shard_map/jkp,mjkc->mjpc/dot_general | solution.py:81
  213.8 6.4 %copy.52 = bf16[2,16,128,512]{3,2,0,1:T(8,128)(2,1)} copy(bf16[2,16,128,512]{2,3,0,1:T(8,128)(2,1)} %convert_bitcast_fusion) | data formatting | bytes 8388608 | tf_op jit(solution)/shard_map/convert_element_type | solution.py:83
  220.2 4.7 %all-to-all-start.1 = ((bf16[2,16,128,512]{3,2,0,1:T(8,128)(2,1)}), bf16[2,16,128,512]{3,2,0,1:T(8,128)(2,1)}, u32[]{:S(2)}, u32[]{:S(2)}) async-start(bf16[2,16,128,512]{3,2,0,1:T(8,128)(2,1)} %copy.52), calls=%async_computation.1 | async-start | bytes 8388608 | tf_op jit(solution)/shard_map/all_to_all | solution.py:84
  225.5 104.7 %psum.15 = f32[]{:T(128)} all-reduce(f32[]{:T(128)} %get-tuple-element.4), channel_id=1, replica_groups=mesh['member'=2,'grid'=16] {'member','grid'}, use_global_device_ids=true, to_apply=%region_6.7 | all-reduce | flops 1 | bytes 8 | tf_op jit(solution)/shard_map/psum | solution.py:63
  330.9 4.7 %fusion.10 = f32[2,16,128,512]{3,1,2,0:T(8,128)S(1)} fusion(bf16[2,16,128,512]{3,2,0,1:T(8,128)(2,1)} %all-to-all-done.1, s32[16]{0:T(128)S(1)} %bitcast.166), kind=kOutput, calls=%fused_computation.20 | convolution fusion | flops 67109120 | bytes 12582976 | tf_op jit(solution)/shard_map/mdpc,db->mbpc/dot_general | solution.py:85
  335.7 8.3 %copy.54 = f32[2,16,128,512]{3,2,1,0:T(8,128)} copy(f32[2,16,128,512]{3,1,2,0:T(8,128)S(1)} %fusion.10) | data formatting | bytes 16777216 | tf_op jit(solution)/shard_map/mdpc,db->mbpc/transpose | solution.py:85
  (22 shorter events, 0.1 us)
Async XLA Ops:
  7.2 117.3 %copy-start = (bf16[512,512]{1,0:T(8,128)(2,1)S(1)}, bf16[512,512]{1,0:T(8,128)(2,1)}, u32[]{:S(2)}) copy-start(bf16[512,512]{1,0:T(8,128)(2,1)} %param.14) | copy-start | bytes 1572868
  12.9 13.6 %copy-start.3 = (bf16[16,2,128,512]{3,2,1,0:T(8,128)(2,1)S(1)}, bf16[16,2,128,512]{3,2,1,0:T(8,128)(2,1)}, u32[]{:S(2)}) copy-start(bf16[16,2,128,512]{3,2,1,0:T(8,128)(2,1)} %gather_fusion) | copy-start | bytes 12582916
  32.3 8.6 %copy-start.5 = (bf16[1,16,128,128]{3,2,1,0:T(8,128)(2,1)S(1)}, bf16[1,16,128,128]{3,2,1,0:T(8,128)(2,1)}, u32[]{:S(2)}) copy-start(bf16[1,16,128,128]{3,2,1,0:T(8,128)(2,1)} %param.11) | copy-start | bytes 1572868
  32.3 88.3 %all-to-all-start = ((bf16[16,2,1,128,512]{4,3,1,2,0:T(8,128)(2,1)}), bf16[16,2,1,128,512]{4,3,1,2,0:T(8,128)(2,1)}, u32[]{:S(2)}, u32[]{:S(2)}) async-start(bf16[16,2,1,128,512]{4,3,1,2,0:T(8,128)(2,1)} %fusion.24), calls=%async_computation | async-start | bytes 8388608 | tf_op jit(solution)/shard_map/all_to_all | solution.py:38
  40.8 146.8 %all-gather.2.cloned.1.call-start = ((), (), s32[]{:S(2)}) async-start(), calls=%async_computation.2 | async-start | bytes 6291456 | tf_op jit(solution)/shard_map/all_gather | solution.py:50
  124.5 2.5 copy-start.9
  124.5 2.5 copy-start.10
  124.5 2.5 copy-start.11
  127.0 4.1 %copy-start.4 = (f32[4096,512]{1,0:T(8,128)}, f32[4096,512]{1,0:T(8,128)S(1)}, u32[]{:S(2)}) copy-start(f32[4096,512]{1,0:T(8,128)S(1)} %fusion.51) | copy-start | bytes 25165828
  127.0 4.1 %copy-start.7 = (s32[1,16]{1,0:T(1,128)S(1)}, s32[1,16]{1,0:T(1,128)}, u32[]{:S(2)}) copy-start(s32[1,16]{1,0:T(1,128)} %param.13) | copy-start | bytes 196
  194.9 1.6 copy-start.2
  194.9 1.8 copy-start.6
  220.2 110.7 %copy-start.8 = (s32[1,16]{1,0:T(1,128)S(1)}, s32[1,16]{1,0:T(1,128)}, u32[]{:S(2)}) copy-start(s32[1,16]{1,0:T(1,128)} %param.10) | copy-start | bytes 196
  220.2 110.7 %all-to-all-start.1 = ((bf16[2,16,128,512]{3,2,0,1:T(8,128)(2,1)}), bf16[2,16,128,512]{3,2,0,1:T(8,128)(2,1)}, u32[]{:S(2)}, u32[]{:S(2)}) async-start(bf16[2,16,128,512]{3,2,0,1:T(8,128)(2,1)} %copy.52), calls=%async_computation.1 | async-start | bytes 8388608 | tf_op jit(solution)/shard_map/all_to_all | solution.py:84
  335.7 8.3 %copy-start.1 = (bf16[512,512]{1,0:T(8,128)(2,1)S(1)}, bf16[512,512]{1,0:T(8,128)(2,1)}, u32[]{:S(2)}) copy-start(bf16[512,512]{1,0:T(8,128)(2,1)} %param.14) | copy-start | bytes 1572868
Sparse Core Ops, SparseCore 0:
  131.2 28.1 all-gather.1
